TPU v7x, 1024 devices: a whole 4x4x32 slice. The times are simulated.
1024 devices in a mesh: dp: 16 (over y, x), expert: 32 (over z), tp: 2 (over core).
Axes of the slice: x: 4, y: 4, z: 32, core: 2. Of those that a mesh axis runs over, the one named last changes fastest.
Arguments:
- tokens: bfloat16 [8192, 2048], P(('dp', 'expert')), may hold values from -24 to 24
- grad_out: bfloat16 [8192, 2048], P(('dp', 'expert')), may hold values from -6 to 6
- expert_ids: int32 [8192, 8], P(('dp', 'expert')), may hold values from 0 to 31, all different within a row; in each aligned block of 16 rows (0 to 15, 16 to 31, ...) at most 6 rows name the same one
- route_probs: bfloat16 [8192, 8], P(('dp', 'expert')), may hold values from 0.049804688 to 1
- w_gate: bfloat16 [32, 2048, 768], P('expert', None, 'tp'), may hold values from -0.125 to 0.125
- w_up: bfloat16 [32, 2048, 768], P('expert', None, 'tp'), may hold values from -0.125 to 0.125
- w_down: bfloat16 [32, 768, 2048], P('expert', 'tp'), may hold values from -0.21875 to 0.21875
Outputs:
- d_tokens: bfloat16 [8192, 2048], P(('dp', 'expert'))
- d_probs: bfloat16 [8192, 8], P(('dp', 'expert'))
- grad_gate: bfloat16 [32, 2048, 768], P('expert', 'dp', 'tp')
- grad_up: bfloat16 [32, 2048, 768], P('expert', 'dp', 'tp')
- grad_down: bfloat16 [32, 768, 2048], P('expert', 'tp', 'dp')
Inputs may be any that keep to these rules, and one draw needn't show every extreme that they name: `expert_ids`: each row names 8 different experts. At most 6 rows of one device's aligned block of 16 rows name one expert, and some block has exactly 6 rows naming one expert.
All inputs are finite; a program needn't handle non-finite values.
Results may differ from a plain program's by a relative error of at most 0.015.
Values may be sent and summed in bfloat16 or wider, within the bound.
No kernel may reach another device: no remote copies, remote signals or barrier semaphores. Data moves between devices by JAX's collectives and lax.ppermute only.
A program may use at most 64 MiB of HBM per device.

v0:
```python
import jax
import jax.numpy as jnp
from jax import lax
from jax.sharding import PartitionSpec as P

CAP = 6


def local(tokens, grad_out, expert_ids, route_probs, w_gate, w_up, w_down):
    tok_count, model_width = tokens.shape
    top_count = expert_ids.shape[1]
    local_count, _, hidden_units = w_gate.shape
    groups = lax.axis_size("expert")
    expert_count = local_count * groups
    capacity = CAP
    slot_count = tok_count * top_count
    place_count = expert_count * capacity
    flat_ids = expert_ids.reshape(slot_count)
    expert_iota = lax.broadcasted_iota(jnp.int32, (slot_count, expert_count), 1)
    chosen = (flat_ids[:, None] == expert_iota).astype(jnp.float32)
    lower = (
        lax.broadcasted_iota(jnp.int32, (slot_count, slot_count), 1)
        < lax.broadcasted_iota(jnp.int32, (slot_count, slot_count), 0)
    ).astype(jnp.float32)
    earlier = jnp.dot(
        lower, chosen, precision=lax.Precision.HIGHEST, preferred_element_type=jnp.float32
    )
    rank = jnp.sum(earlier * chosen, axis=1).astype(jnp.int32)
    position = flat_ids * capacity + rank
    placed = position[:, None] == lax.broadcasted_iota(jnp.int32, (slot_count, place_count), 1)
    place_f32 = placed.astype(jnp.float32)
    token_map = jnp.any(placed.reshape(tok_count, top_count, place_count), axis=1).astype(
        jnp.bfloat16
    )
    send_x = jnp.einsum("tp,td->pd", token_map, tokens, preferred_element_type=jnp.float32)
    send_dy = jnp.einsum("tp,td->pd", token_map, grad_out, preferred_element_type=jnp.float32)
    send_p = jnp.einsum(
        "sp,s->p",
        place_f32,
        route_probs.reshape(slot_count).astype(jnp.float32),
        precision=lax.Precision.HIGHEST,
    )
    send_x = send_x.astype(jnp.bfloat16).reshape(expert_count, capacity, model_width)
    send_dy = send_dy.astype(jnp.bfloat16).reshape(expert_count, capacity, model_width)
    send_p = send_p.astype(jnp.bfloat16).reshape(expert_count, capacity)
    recv_x, recv_dy, recv_p = (
        lax.all_to_all(send_x, "expert", split_axis=0, concat_axis=1, tiled=True),
        lax.all_to_all(send_dy, "expert", split_axis=0, concat_axis=1, tiled=True),
        lax.all_to_all(send_p, "expert", split_axis=0, concat_axis=1, tiled=True),
    )
    gate = jnp.einsum("erd,edf->erf", recv_x, w_gate, preferred_element_type=jnp.float32)
    up_val = jnp.einsum("erd,edf->erf", recv_x, w_up, preferred_element_type=jnp.float32)
    silu_gate = jax.nn.silu(gate)
    hidden = (silu_gate * up_val).astype(jnp.bfloat16)
    back = jnp.einsum("erd,efd->erf", recv_dy, w_down, preferred_element_type=jnp.float32)
    prob_part = jnp.sum(hidden.astype(jnp.float32) * back, axis=2)
    weight = recv_p.astype(jnp.float32)[..., None]
    d_hidden = weight * back
    sigma = jax.nn.sigmoid(gate)
    d_gate = (d_hidden * up_val * sigma * (1.0 + gate * (1.0 - sigma))).astype(jnp.bfloat16)
    d_up = (d_hidden * silu_gate).astype(jnp.bfloat16)
    row_part = jnp.einsum(
        "erf,edf->erd", d_gate, w_gate, preferred_element_type=jnp.float32
    ) + jnp.einsum("erf,edf->erd", d_up, w_up, preferred_element_type=jnp.float32)
    scaled = (weight * recv_dy.astype(jnp.float32)).astype(jnp.bfloat16)
    row_sum, prob_sum = (
        lax.psum(row_part.astype(jnp.bfloat16), "tp").astype(jnp.float32),
        lax.psum(prob_part.astype(jnp.bfloat16), "tp").astype(jnp.float32),
    )
    back_rows, back_prob = (
        lax.all_to_all(
            row_sum.astype(jnp.bfloat16), "expert", split_axis=1, concat_axis=0, tiled=True
        ),
        lax.all_to_all(
            prob_sum.astype(jnp.bfloat16), "expert", split_axis=1, concat_axis=0, tiled=True
        ),
    )
    column_count = back_rows.shape[2]
    summed = jnp.dot(
        token_map, back_rows.reshape(place_count, column_count), preferred_element_type=jnp.float32
    ).astype(jnp.bfloat16)
    prob_grad = jnp.einsum(
        "sp,p->s",
        place_f32,
        back_prob.reshape(place_count).astype(jnp.float32),
        precision=lax.Precision.HIGHEST,
    )
    d_probs = prob_grad.reshape(tok_count, top_count).astype(jnp.bfloat16)
    share = model_width // lax.axis_size("dp")
    gate_term = jnp.einsum("erd,erf->def", recv_x, d_gate, preferred_element_type=jnp.float32)
    up_term = jnp.einsum("erd,erf->def", recv_x, d_up, preferred_element_type=jnp.float32)
    down_term = jnp.einsum("erd,erf->def", scaled, hidden, preferred_element_type=jnp.float32)
    joined = jnp.concatenate([gate_term, up_term, down_term], axis=1)
    grad_sum = lax.psum_scatter(
        joined.reshape(share * lax.axis_size("dp"), 3 * local_count * hidden_units).astype(
            jnp.bfloat16
        ),
        "dp",
        scatter_dimension=0,
        tiled=True,
    ).astype(jnp.float32)
    grad_parts = grad_sum.reshape(share, 3, local_count, hidden_units).astype(jnp.bfloat16)
    grad_gate = jnp.transpose(grad_parts[:, 0], (1, 0, 2))
    grad_up = jnp.transpose(grad_parts[:, 1], (1, 0, 2))
    grad_down = jnp.transpose(grad_parts[:, 2], (1, 2, 0))
    return (summed, d_probs, grad_gate, grad_up, grad_down)


def solution(mesh):
    return jax.shard_map(
        local,
        mesh=mesh,
        in_specs=(
            P(("dp", "expert"), None),
            P(("dp", "expert"), None),
            P(("dp", "expert"), None),
            P(("dp", "expert"), None),
            P("expert", None, "tp"),
            P("expert", None, "tp"),
            P("expert", "tp", None),
        ),
        out_specs=(
            P(("dp", "expert"), None),
            P(("dp", "expert"), None),
            P("expert", "dp", "tp"),
            P("expert", "dp", "tp"),
            P("expert", "tp", "dp"),
        ),
        check_vma=False,
    )
```

profile of v0, /device:TPU:1, one launch (start us, length us, event | category | flops | bytes accessed | tf_op | source)
XLA Modules:
  0.0 475.9 jit_solution(15800634043784314238)
XLA Ops:
  11.0 29.3 %all-to-all-start = ((bf16[32,1,6]{2,1,0:T(2,128)(2,1)}), bf16[32,1,6]{2,1,0:T(2,128)(2,1)S(1)}, u32[]{:S(2)}, u32[]{:S(2)}) async-start(bf16[32,1,6]{2,1,0:T(2,128)(2,1)} %all_to_all.23), calls=%async_computation | async-start | bytes 32768 | tf_op jit(solution)/shard_map/all_to_all | solution.py:49
  41.7 1.3 reshape.230
  43.0 18.4 %all-to-all-done = bf16[32,1,6]{2,1,0:T(2,128)(2,1)S(1)} async-done(((bf16[32,1,6]{2,1,0:T(2,128)(2,1)}), bf16[32,1,6]{2,1,0:T(2,128)(2,1)S(1)}, u32[]{:S(2)}, u32[]{:S(2)}) %all-to-all-start) | async-done | bytes 416 | tf_op jit(solution)/shard_map/all_to_all | solution.py:49
  61.5 3.9 all-to-all-start.2
  65.8 1.2 reshape.227
  67.1 103.7 %all-to-all-done.2 = bf16[32,6,2048]{2,1,0:T(8,128)(2,1)S(1)} async-done(((bf16[32,6,2048]{2,1,0:T(8,128)(2,1)}), bf16[32,6,2048]{2,1,0:T(8,128)(2,1)S(1)}, u32[]{:S(2)}, u32[]{:S(2)}) %all-to-all-start.2) | async-done | bytes 786464 | tf_op jit(solution)/shard_map/all_to_all | solution.py:47
  170.8 7.2 %all-to-all-start.1 = ((bf16[32,6,2048]{2,1,0:T(8,128)(2,1)}), bf16[32,6,2048]{2,1,0:T(8,128)(2,1)}, u32[]{:S(2)}, u32[]{:S(2)}) async-start(bf16[32,6,2048]{2,1,0:T(8,128)(2,1)} %reshape.227), calls=%async_computation.1 | async-start | bytes 2097152 | tf_op jit(solution)/shard_map/all_to_all | solution.py:48
  178.5 2.7 fusion.10
  181.2 1.3 fusion.7
  182.5 100.6 %all-to-all-done.1 = bf16[32,6,2048]{2,1,0:T(8,128)(2,1)} async-done(((bf16[32,6,2048]{2,1,0:T(8,128)(2,1)}), bf16[32,6,2048]{2,1,0:T(8,128)(2,1)}, u32[]{:S(2)}, u32[]{:S(2)}) %all-to-all-start.1) | async-done | bytes 786464 | tf_op jit(solution)/shard_map/all_to_all | solution.py:48
  283.1 1.4 reshape.228
  284.5 2.9 multiply_reduce_fusion
  288.8 1.6 fusion.4
  292.7 2.4 pad_maximum_fusion
  295.2 6.8 %copy.49 = bf16[2048,1152]{1,0:T(8,128)(2,1)} copy(bf16[2048,1152]{0,1:T(8,128)(2,1)} %bitcast.69) | data formatting | bytes 9437184
  302.1 3.7 psum.15
  306.4 6.7 %all-to-all-start.4 = ((bf16[1,32,6]{2,0,1:T(2,128)(2,1)}), bf16[1,32,6]{2,0,1:T(2,128)(2,1)S(1)}, u32[]{:S(2)}, u32[]{:S(2)}) async-start(bf16[1,32,6]{2,0,1:T(2,128)(2,1)} %copy.45), calls=%async_computation.4 | async-start | bytes 32768 | tf_op jit(solution)/shard_map/all_to_all | solution.py:74
  313.1 27.5 %all-reduce.2.cloned.1.call-done = bf16[1,192,2048]{2,1,0:T(8,128)(2,1)} async-done(((bf16[1,192,2048]{2,1,0:T(8,128)(2,1)}), bf16[1,192,2048]{2,1,0:T(8,128)(2,1)}) %all-reduce.2.cloned.1.call-update) | async-done | bytes 786448 | tf_op jit(solution)/shard_map/psum | solution.py:67
  340.6 2.4 copy.57
  343.5 6.2 %reduce.7 = bf16[192,2048]{1,0:T(8,128)(2,1)} reduce(bf16[192,1,2048]{2,1,0:T(2,128)(2,1)S(1)} %bitcast.70, bf16[]{:T(256)} %broadcast.60), dimensions={1}, to_apply=%bitcast.68.reduce_sub_computation | reduce | bytes 1572866
  349.7 3.0 reshape.254
  352.7 20.3 %all-to-all-start.3 = ((bf16[32,2,6144]{2,1,0:T(2,128)(2,1)}), bf16[32,2,6144]{2,1,0:T(2,128)(2,1)}, u32[]{:S(2)}, u32[]{:S(2)}) async-start(bf16[32,2,6144]{2,1,0:T(2,128)(2,1)} %reshape.254), calls=%async_computation.3 | async-start | bytes 1572864 | tf_op jit(solution)/shard_map/all_to_all | solution.py:71
  374.1 85.0 %all-to-all-done.3 = bf16[32,2,6144]{2,1,0:T(2,128)(2,1)} async-done(((bf16[32,2,6144]{2,1,0:T(2,128)(2,1)}), bf16[32,2,6144]{2,1,0:T(2,128)(2,1)}, u32[]{:S(2)}, u32[]{:S(2)}) %all-to-all-start.3) | async-done | bytes 786464 | tf_op jit(solution)/shard_map/all_to_all | solution.py:71
  459.1 4.9 %reshape.255 = bf16[192,1,2048]{2,1,0:T(2,128)(2,1)S(1)} reshape(bf16[32,2,6144]{2,1,0:T(2,128)(2,1)} %all-to-all-done.3) | data formatting | bytes 1572864
  (48 shorter events, 15.8 us)
Async XLA Ops:
  8.0 173.2 %copy-start = (bf16[1,2048,384]{2,1,0:T(8,128)(2,1)S(1)}, bf16[1,2048,384]{2,1,0:T(8,128)(2,1)}, u32[]{:S(2)}) copy-start(bf16[1,2048,384]{2,1,0:T(8,128)(2,1)} %param.11) | copy-start | bytes 4718596
  11.0 50.5 %all-to-all-start = ((bf16[32,1,6]{2,1,0:T(2,128)(2,1)}), bf16[32,1,6]{2,1,0:T(2,128)(2,1)S(1)}, u32[]{:S(2)}, u32[]{:S(2)}) async-start(bf16[32,1,6]{2,1,0:T(2,128)(2,1)} %all_to_all.23), calls=%async_computation | async-start | bytes 32768 | tf_op jit(solution)/shard_map/all_to_all | solution.py:49
  41.7 23.7 %copy-start.3 = (bf16[16,2048]{1,0:T(8,128)(2,1)S(1)}, bf16[16,2048]{1,0:T(8,128)(2,1)}, u32[]{:S(2)}) copy-start(bf16[16,2048]{1,0:T(8,128)(2,1)} %param.8) | copy-start | bytes 196612
  61.5 109.3 %all-to-all-start.2 = ((bf16[32,6,2048]{2,1,0:T(8,128)(2,1)}), bf16[32,6,2048]{2,1,0:T(8,128)(2,1)S(1)}, u32[]{:S(2)}, u32[]{:S(2)}) async-start(bf16[32,6,2048]{2,1,0:T(8,128)(2,1)} %reshape.230), calls=%async_computation.2 | async-start | bytes 2097152 | tf_op jit(solution)/shard_map/all_to_all | solution.py:47
  170.8 112.3 %all-to-all-start.1 = ((bf16[32,6,2048]{2,1,0:T(8,128)(2,1)}), bf16[32,6,2048]{2,1,0:T(8,128)(2,1)}, u32[]{:S(2)}, u32[]{:S(2)}) async-start(bf16[32,6,2048]{2,1,0:T(8,128)(2,1)} %reshape.227), calls=%async_computation.1 | async-start | bytes 2097152 | tf_op jit(solution)/shard_map/all_to_all | solution.py:48
  178.0 162.6 %all-reduce.2.cloned.1.call-start = ((), (), s32[]{:S(2)}) async-start(), calls=%async_computation.6 | async-start | bytes 1572864 | tf_op jit(solution)/shard_map/psum | solution.py:67
  287.4 1.4 copy-start.1
  290.5 174.6 %reduce-scatter.4.cloned.1.call-start = ((), (), s32[]{:S(2)}) async-start(), calls=%async_computation.7 | async-start | bytes 5013504
  291.2 0.9 copy-start.2
  306.4 46.3 %all-to-all-start.4 = ((bf16[1,32,6]{2,0,1:T(2,128)(2,1)}), bf16[1,32,6]{2,0,1:T(2,128)(2,1)S(1)}, u32[]{:S(2)}, u32[]{:S(2)}) async-start(bf16[1,32,6]{2,0,1:T(2,128)(2,1)} %copy.45), calls=%async_computation.4 | async-start | bytes 32768 | tf_op jit(solution)/shard_map/all_to_all | solution.py:74
  352.7 106.4 %all-to-all-start.3 = ((bf16[32,2,6144]{2,1,0:T(2,128)(2,1)}), bf16[32,2,6144]{2,1,0:T(2,128)(2,1)}, u32[]{:S(2)}, u32[]{:S(2)}) async-start(bf16[32,2,6144]{2,1,0:T(2,128)(2,1)} %reshape.254), calls=%async_computation.3 | async-start | bytes 1572864 | tf_op jit(solution)/shard_map/all_to_all | solution.py:71
Sparse Core Ops, SparseCore 0:
  290.6 49.9 all-reduce.1
Sparse Core Ops, SparseCore 1:
  302.1 99.7 reduce-scatter.3
where the time goes:
time: 477 us; the launch traced here: 476 us
  waiting for transfers between devices  335 us (70%)
  starting transfers between devices  67.5 us (14%)
  local copies, waits for them, and re-layouts  30.4 us (6%)
  between operations  15.7 us (3%)
  matrix products  14.6 us (3%)
  other arithmetic  8.9 us (2%)
    all_to_all x1, waiting for transfers between devices, local(): lax.all_to_all(send_x, 'expert', split_axis=0, concat_axis=1, tiled=True)  104 us
    all_to_all x1, waiting for transfers between devices, local(): lax.all_to_all(send_dy, 'expert', split_axis=0, concat_axis=1, tiled=True)  101 us
    all_to_all x1, waiting for transfers between devices, local(): lax.all_to_all(row_sum.astype(jnp.bfloat16), 'expert', split_axis=1, conc...  85 us
    all_to_all x1, starting transfers between devices, local(): lax.all_to_all(send_p, 'expert', split_axis=0, concat_axis=1, tiled=True)  29.3 us
    psum x1, waiting for transfers between devices, local(): lax.psum(row_part.astype(jnp.bfloat16), 'tp').astype(jnp.float32)  27.5 us
    all_to_all x1, starting transfers between devices, local(): lax.all_to_all(row_sum.astype(jnp.bfloat16), 'expert', split_axis=1, conc...  20.3 us
    unnamed x15, local copies, waits for them, and re-layouts  19 us
    all_to_all x1, waiting for transfers between devices, local(): lax.all_to_all(send_p, 'expert', split_axis=0, concat_axis=1, tiled=True)  18.4 us
  transfers between devices with their start and end apart: 7, of which 5 were waited for; matrix products, arithmetic and copies ran while one was open for 8% of the time, Pallas kernels for 0%

commit v1 on v0

v1 whole, which is shorter than its diff:
```python
import jax
import jax.numpy as jnp
from jax import lax
from jax.sharding import PartitionSpec as P

CAP = 6
ROWS = 8
F32 = jnp.float32
BF16 = jnp.bfloat16
SWAP = [(0, 1), (1, 0)]


def dot(a, b, ca, cb):
    return lax.dot_general(a, b, (((ca,), (cb,)), ((), ())), preferred_element_type=F32)


def local(tokens, grad_out, expert_ids, route_probs, w_gate, w_up, w_down):
    toks, width = tokens.shape
    top = expert_ids.shape[1]
    groups = lax.axis_size("expert")
    half = width // 2
    hidden_units = w_gate.shape[2]
    core = lax.axis_index("tp")
    first = core == 0
    wg, wu, wd = w_gate[0], w_up[0], w_down[0]

    n = toks * top
    slots = groups * ROWS
    flat = expert_ids.reshape(n)
    chosen = (flat[:, None] == lax.broadcasted_iota(jnp.int32, (n, groups), 1)).astype(BF16)
    lower = (
        lax.broadcasted_iota(jnp.int32, (n, n), 1) < lax.broadcasted_iota(jnp.int32, (n, n), 0)
    ).astype(BF16)
    rank = jnp.sum(dot(lower, chosen, 1, 0) * chosen.astype(F32), axis=1).astype(jnp.int32)
    placed = (flat * ROWS + rank)[:, None] == lax.broadcasted_iota(jnp.int32, (n, slots), 1)
    token_map = jnp.any(placed.reshape(toks, top, slots), axis=1).astype(BF16)

    x_half = jnp.where(first, tokens[:, :half], tokens[:, half:])
    dy_half = jnp.where(first, grad_out[:, :half], grad_out[:, half:])
    rows_sent = dot(token_map, jnp.concatenate([x_half, dy_half], axis=1), 0, 0).astype(BF16)
    at_rank = (rank[:, None] == lax.broadcasted_iota(jnp.int32, (n, 128), 1)).astype(F32)
    weight_at = (at_rank * route_probs.reshape(n, 1).astype(F32)).astype(BF16)
    weights_sent = dot(chosen, weight_at, 0, 0).astype(BF16)
    weights_sent = jnp.pad(weights_sent[:, None, :], ((0, 0), (0, 0), (0, 2 * half - 128)))
    spare = lax.broadcasted_iota(jnp.int32, (1, ROWS, 1), 1) == ROWS - 1
    sent = jnp.where(spare, weights_sent, rows_sent.reshape(groups, ROWS, 2 * half))
    recv = lax.all_to_all(sent, "expert", split_axis=0, concat_axis=0, tiled=True)
    weight = recv[:, ROWS - 1, :ROWS].astype(F32).reshape(slots, 1)
    used = lax.broadcasted_iota(jnp.int32, (slots, 1), 0) % ROWS < CAP
    weight = jnp.where(used, weight, 0.0)
    picked = jnp.where(used, recv.reshape(slots, 2 * half), jnp.zeros((), BF16))
    other = lax.ppermute(picked, "tp", SWAP)
    low, high = jnp.where(first, picked, other), jnp.where(first, other, picked)
    x = jnp.concatenate([low[:, :half], high[:, :half]], axis=1)
    dy = jnp.concatenate([low[:, half:], high[:, half:]], axis=1)

    gate = dot(x, wg, 1, 0)
    up = dot(x, wu, 1, 0)
    silu_gate = jax.nn.silu(gate)
    hidden = (silu_gate * up).astype(BF16)
    back = dot(dy, wd, 1, 1)
    prob_part = jnp.sum(hidden.astype(F32) * back, axis=1)
    d_hidden = weight * back
    sigma = jax.nn.sigmoid(gate)
    d_gate = (d_hidden * up * sigma * (1.0 + gate * (1.0 - sigma))).astype(BF16)
    d_up = (d_hidden * silu_gate).astype(BF16)
    row_part = dot(d_gate, wg, 1, 1) + dot(d_up, wu, 1, 1)
    scaled = (weight * dy.astype(F32)).astype(BF16)

    dp = lax.axis_size("dp")
    joined = jnp.concatenate(
        [
            dot(x, jnp.concatenate([d_gate, d_up], axis=1), 0, 0).astype(BF16),
            dot(scaled, hidden, 0, 0).astype(BF16),
        ],
        axis=1,
    )
    parts = lax.all_to_all(
        joined.reshape(dp, width // dp, 3 * hidden_units), "dp", split_axis=0, concat_axis=0,
        tiled=True,
    )
    grads = jnp.sum(parts.astype(F32), axis=0).astype(BF16)
    sums = [grads[:, i * hidden_units : (i + 1) * hidden_units] for i in range(3)]

    mine = jnp.where(first, row_part[:, :half], row_part[:, half:])
    yours = jnp.where(first, row_part[:, half:], row_part[:, :half])
    prob_pad = jnp.pad(prob_part.astype(BF16)[:, None], ((0, 0), (0, 127)))
    swapped = lax.ppermute(
        jnp.concatenate([yours.astype(BF16), prob_pad], axis=1), "tp", SWAP
    )
    d_row = (mine + swapped[:, :half].astype(F32)).astype(BF16)
    prob = (prob_part.astype(BF16).astype(F32) + swapped[:, half].astype(F32)).astype(BF16)
    prob_rows = prob.reshape(groups, ROWS)[:, None, :]
    prob_rows = jnp.pad(prob_rows, ((0, 0), (0, 0), (0, half - ROWS)))
    back_sent = jnp.where(spare, prob_rows, d_row.reshape(groups, ROWS, half))
    back_recv = lax.all_to_all(back_sent, "expert", split_axis=0, concat_axis=0, tiled=True)

    summed = dot(token_map, back_recv.reshape(slots, half), 1, 0).astype(BF16)
    summed_other = lax.ppermute(summed, "tp", SWAP)
    d_tokens = jnp.where(
        first,
        jnp.concatenate([summed, summed_other], axis=1),
        jnp.concatenate([summed_other, summed], axis=1),
    )
    prob_back = back_recv[:, ROWS - 1, :ROWS].astype(F32)
    by_expert = dot(chosen, prob_back.astype(BF16), 1, 0)
    rank_is = rank[:, None] == lax.broadcasted_iota(jnp.int32, (n, ROWS), 1)
    d_probs = jnp.sum(jnp.where(rank_is, by_expert, 0.0), axis=1).reshape(toks, top).astype(BF16)

    return (d_tokens, d_probs, sums[0][None], sums[1][None], sums[2].T[None])


def solution(mesh):
    return jax.shard_map(
        local,
        mesh=mesh,
        in_specs=(
            P(("dp", "expert"), None),
            P(("dp", "expert"), None),
            P(("dp", "expert"), None),
            P(("dp", "expert"), None),
            P("expert", None, "tp"),
            P("expert", None, "tp"),
            P("expert", "tp", None),
        ),
        out_specs=(
            P(("dp", "expert"), None),
            P(("dp", "expert"), None),
            P("expert", "dp", "tp"),
            P("expert", "dp", "tp"),
            P("expert", "tp", "dp"),
        ),
        check_vma=False,
    )
```

time: 477 us -> 311 us (0.65)
  waiting for transfers between devices: 335 us -> 228 us
  local copies, waits for them, and re-layouts: 30.4 us -> 8.68 us
  starting transfers between devices: 67.5 us -> 52.1 us
  between operations: 15.7 us -> 0.94 us
  matrix products: 14.6 us -> 7.74 us
    all_to_all x5 -> x3, waiting for transfers between devices: 308 us -> 224 us  [the longest x1 105 us: local(): lax.all_to_all(sent, 'expert', split_axis=0, concat_axis=0, tiled=True)]
    psum x1 -> x0, waiting for transfers between devices: 27.5 us -> none  [local(): lax.psum(row_part.astype(jnp.bfloat16), 'tp').astype(jnp.float32)]
    all_to_all x5 -> x3, starting transfers between devices: 67.4 us -> 43.1 us  [the longest x1 29.3 us: local(): lax.all_to_all(sent, 'expert', split_axis=0, concat_axis=0, tiled=True)]
    unnamed x15 -> x14, local copies, waits for them, and re-layouts: 19 us -> 4.79 us
    ppermute x0 -> x3, starting transfers between devices: none -> 8.92 us  [the longest x1 3.38 us: local(): summed_other = lax.ppermute(summed, 'tp', SWAP)]
    dot_general x14 -> x12, matrix products: 14.6 us -> 7.74 us  [dot(): lax.dot_general(a, b, (((ca,), (cb,)), ((), ())), preferred_element_type=...]
    select_n x0 -> x6, other arithmetic: none -> 6.71 us  [the longest x1 2.68 us: local(): back_sent = jnp.where(spare, prob_rows, d_row.reshape(groups, ROWS, half))]
    unnamed x1 -> x0, other arithmetic: 6.19 us -> none
  transfers between devices with their start and end apart: 7 -> 6, of which waited for: 5 -> 5; matrix products, arithmetic and copies ran while one was open for 8% -> 4% of each run, Pallas kernels for 0% -> 0%
where the time goes in v1:
time: 311 us
  waiting for transfers between devices  228 us (73%)
  starting transfers between devices  52.1 us (17%)
  other arithmetic  12.9 us (4%)
  local copies, waits for them, and re-layouts  8.68 us (3%)
  matrix products  7.74 us (2%)
    all_to_all x1, waiting for transfers between devices, local(): lax.all_to_all(sent, 'expert', split_axis=0, concat_axis=0, tiled=True)  105 us
    all_to_all x1, waiting for transfers between devices, local(): lax.all_to_all(joined.reshape(dp, width // dp, 3 * hidden_units), 'dp', s...  60.2 us
    all_to_all x1, waiting for transfers between devices, local(): lax.all_to_all(back_sent, 'expert', split_axis=0, concat_axis=0, tiled=True)  59.1 us
    all_to_all x1, starting transfers between devices, local(): lax.all_to_all(sent, 'expert', split_axis=0, concat_axis=0, tiled=True)  29.3 us
    dot_general x12, matrix products, dot(): lax.dot_general(a, b, (((ca,), (cb,)), ((), ())), preferred_element_type=...  7.74 us
    all_to_all x1, starting transfers between devices, local(): lax.all_to_all(back_sent, 'expert', split_axis=0, concat_axis=0, tiled=True)  7.07 us
    all_to_all x1, starting transfers between devices, local(): lax.all_to_all(joined.reshape(dp, width // dp, 3 * hidden_units), 'dp', s...  6.8 us
  transfers between devices with their start and end apart: 6, of which 5 were waited for; matrix products, arithmetic and copies ran while one was open for 4% of the time, Pallas kernels for 0%

profile of v1, /device:TPU:1, one launch (start us, length us, event | category | flops | bytes accessed | tf_op | source)
XLA Modules:
  0.0 310.6 jit_solution(11611809976006835960)
XLA Ops:
  0.7 0.9 copy.42
  2.0 0.8 copy.44
  3.1 0.8 slice_select_fusion
  4.0 1.5 fusion.1
  5.4 29.3 %all-to-all-start = ((bf16[32,8,2048]{2,1,0:T(8,128)(2,1)}), bf16[32,8,2048]{2,1,0:T(8,128)(2,1)S(1)}, u32[]{:S(2)}, u32[]{:S(2)}) async-start(bf16[32,8,2048]{2,1,0:T(8,128)(2,1)} %fusion.1), calls=%async_computation | async-start | bytes 2097152 | tf_op jit(solution)/shard_map/all_to_all | solution.py:47
  34.7 105.0 %all-to-all-done = bf16[32,8,2048]{2,1,0:T(8,128)(2,1)S(1)} async-done(((bf16[32,8,2048]{2,1,0:T(8,128)(2,1)}), bf16[32,8,2048]{2,1,0:T(8,128)(2,1)S(1)}, u32[]{:S(2)}, u32[]{:S(2)}) %all-to-all-start) | async-done | bytes 1048608 | tf_op jit(solution)/shard_map/all_to_all | solution.py:47
  139.7 1.1 bitcast_select_fusion
  140.8 3.0 collective-permute-start
  144.0 2.4 collective-permute-done
  146.4 1.4 broadcast_select_fusion.1
  148.0 1.2 copy-done.2
  151.4 0.9 multiply_reduce_fusion
  153.0 1.0 convolution_convert_fusion
  154.1 2.6 copy_bitcast_fusion
  156.7 6.8 %all-to-all-start.2 = ((bf16[16,128,1152]{1,2,0:T(8,128)(2,1)}), bf16[16,128,1152]{1,2,0:T(8,128)(2,1)}, u32[]{:S(2)}, u32[]{:S(2)}) async-start(bf16[16,128,1152]{1,2,0:T(8,128)(2,1)} %copy_bitcast_fusion), calls=%async_computation.2 | async-start | bytes 9437184 | tf_op jit(solution)/shard_map/all_to_all | solution.py:78
  165.1 1.3 copy-done.1
  166.6 2.6 collective-permute-start.1
  169.2 1.5 collective-permute-done.1
  171.0 2.7 fusion.18
  173.7 60.2 %all-to-all-done.2 = bf16[16,128,1152]{1,2,0:T(8,128)(2,1)} async-done(((bf16[16,128,1152]{1,2,0:T(8,128)(2,1)}), bf16[16,128,1152]{1,2,0:T(8,128)(2,1)}, u32[]{:S(2)}, u32[]{:S(2)}) %all-to-all-start.2) | async-done | bytes 4718624 | tf_op jit(solution)/shard_map/all_to_all | solution.py:78
  233.9 7.1 %all-to-all-start.1 = ((bf16[32,8,1024]{2,1,0:T(8,128)(2,1)}), bf16[32,8,1024]{2,1,0:T(8,128)(2,1)S(1)}, u32[]{:S(2)}, u32[]{:S(2)}) async-start(bf16[32,8,1024]{2,1,0:T(8,128)(2,1)} %fusion.18), calls=%async_computation.1 | async-start | bytes 1048576 | tf_op jit(solution)/shard_map/all_to_all | solution.py:96
  240.9 3.1 %reduce_sum.42 = bf16[128,1152]{0,1:T(8,128)(2,1)S(1)} reduce(bf16[16,128,1152]{1,2,0:T(8,128)(2,1)} %all-to-all-done.2, bf16[]{:T(256)} %constant.36.clone.1), dimensions={0}, to_apply=%region_4.5 | reduce | flops 2211840 | bytes 5013506 | tf_op jit(solution)/shard_map/reduce_sum | solution.py:82
  246.2 59.1 %all-to-all-done.1 = bf16[32,8,1024]{2,1,0:T(8,128)(2,1)S(1)} async-done(((bf16[32,8,1024]{2,1,0:T(8,128)(2,1)}), bf16[32,8,1024]{2,1,0:T(8,128)(2,1)S(1)}, u32[]{:S(2)}, u32[]{:S(2)}) %all-to-all-start.1) | async-done | bytes 524320 | tf_op jit(solution)/shard_map/all_to_all | solution.py:96
  305.5 3.4 %collective-permute-start.2 = (bf16[16,1024]{1,0:T(8,128)(2,1)S(1)}, bf16[16,1024]{1,0:T(8,128)(2,1)S(1)}, u32[]{:S(2)}, u32[]{:S(2)}) collective-permute-start(bf16[16,1024]{1,0:T(8,128)(2,1)S(1)} %convolution_convert_fusion.3), channel_id=1, source_target_pairs={{0,1},{1,0},{2,3},{3,2},{4,5},{5,4},{6,7},{7,6},{8,9},{9,8},{10,11... | collective-permute-start | bytes 98312 | tf_op jit(solution)/shard_map/ppermute | solution.py:99
  (50 shorter events, 10.0 us)
Async XLA Ops:
  0.6 149.4 %copy-start = (bf16[1,2048,384]{2,1,0:T(8,128)(2,1)S(1)}, bf16[1,2048,384]{2,1,0:T(8,128)(2,1)}, u32[]{:S(2)}) copy-start(bf16[1,2048,384]{2,1,0:T(8,128)(2,1)} %param.11) | copy-start | bytes 4718596
  1.8 3.6 %copy-start.3 = (s32[128]{0:T(128)}, s32[128]{0:T(128)S(1)}, u32[]{:S(2)}) copy-start(s32[128]{0:T(128)S(1)} %convert_element_type.165) | copy-start | bytes 1540
  5.4 134.3 %all-to-all-start = ((bf16[32,8,2048]{2,1,0:T(8,128)(2,1)}), bf16[32,8,2048]{2,1,0:T(8,128)(2,1)S(1)}, u32[]{:S(2)}, u32[]{:S(2)}) async-start(bf16[32,8,2048]{2,1,0:T(8,128)(2,1)} %fusion.1), calls=%async_computation | async-start | bytes 2097152 | tf_op jit(solution)/shard_map/all_to_all | solution.py:47
  140.8 5.6 %collective-permute-start = (bf16[256,2048]{1,0:T(8,128)(2,1)}, bf16[256,2048]{1,0:T(8,128)(2,1)}, u32[]{:S(2)}, u32[]{:S(2)}) collective-permute-start(bf16[256,2048]{1,0:T(8,128)(2,1)} %bitcast_select_fusion), channel_id=1, source_target_pairs={{0,1},{1,0},{2,3},{3,2},{4,5},{5,4},{6,7},{7,6},{8,9},{9,8},{10,11... | collective-permute-start | bytes 3145736 | tf_op jit(solution)/shard_map/ppermute | solution.py:52
  147.8 1.4 copy-start.2
  150.0 1.4 copy-start.5
  156.7 77.2 %all-to-all-start.2 = ((bf16[16,128,1152]{1,2,0:T(8,128)(2,1)}), bf16[16,128,1152]{1,2,0:T(8,128)(2,1)}, u32[]{:S(2)}, u32[]{:S(2)}) async-start(bf16[16,128,1152]{1,2,0:T(8,128)(2,1)} %copy_bitcast_fusion), calls=%async_computation.2 | async-start | bytes 9437184 | tf_op jit(solution)/shard_map/all_to_all | solution.py:78
  165.1 1.3 copy-start.1
  166.6 4.2 %collective-permute-start.1 = (bf16[256,1152]{1,0:T(8,128)(2,1)S(1)}, bf16[256,1152]{1,0:T(8,128)(2,1)S(1)}, u32[]{:S(2)}, u32[]{:S(2)}) collective-permute-start(bf16[256,1152]{1,0:T(8,128)(2,1)S(1)} %fusion.16), channel_id=1, source_target_pairs={{0,1},{1,0},{2,3},{3,2},{4,5},{5,4},{6,7},{7,6},{8,9},{9,8},{10,11... | collective-permute-start | bytes 1769480 | tf_op jit(solution)/shard_map/ppermute | solution.py:88
  233.9 71.5 %all-to-all-start.1 = ((bf16[32,8,1024]{2,1,0:T(8,128)(2,1)}), bf16[32,8,1024]{2,1,0:T(8,128)(2,1)S(1)}, u32[]{:S(2)}, u32[]{:S(2)}) async-start(bf16[32,8,1024]{2,1,0:T(8,128)(2,1)} %fusion.18), calls=%async_computation.1 | async-start | bytes 1048576 | tf_op jit(solution)/shard_map/all_to_all | solution.py:96
  240.9 68.1 %copy-start.4 = (s32[128]{0:T(128)S(1)}, s32[128]{0:T(128)}, u32[]{:S(2)}) copy-start(s32[128]{0:T(128)} %copy-done.3) | copy-start | bytes 1540
  305.5 4.4 %collective-permute-start.2 = (bf16[16,1024]{1,0:T(8,128)(2,1)S(1)}, bf16[16,1024]{1,0:T(8,128)(2,1)S(1)}, u32[]{:S(2)}, u32[]{:S(2)}) collective-permute-start(bf16[16,1024]{1,0:T(8,128)(2,1)S(1)} %convolution_convert_fusion.3), channel_id=1, source_target_pairs={{0,1},{1,0},{2,3},{3,2},{4,5},{5,4},{6,7},{7,6},{8,9},{9,8},{10,11... | collective-permute-start | bytes 98312 | tf_op jit(solution)/shard_map/ppermute | solution.py:99
